TPU v7x, 32 devices: a whole 2x2x4 slice. The times are simulated.
32 devices in a mesh: group: 4 (over x, core), dev: 8 (over z, y).
Axes of the slice: x: 2, y: 2, z: 4, core: 2. Of those that a mesh axis runs over, the one named last changes fastest.
Arguments:
- adjoint_seed: bfloat16 [64, 3, 48, 16, 128], P(('group', 'dev')), may hold values from -6 to 6
- stiffness: float32 [64, 48, 16, 128], P(('group', 'dev')), may hold values from 0.1 to 0.4
- lengths: int32 [64], P(('group', 'dev')), may hold values from 24 to 48, as said below
- conn_lower: int32 [64, 3], P(('group', 'dev')), may hold values from -1 to 7, as said below
- conn_upper: int32 [64, 3], P(('group', 'dev')), may hold values from -1 to 7, as said below
- coord_x: float32 [64, 48], P(('group', 'dev')), may hold values from 0 to 95
- coord_y: float32 [64, 16], P(('group', 'dev')), may hold values from 0 to 63
- coord_z: float32 [64, 128], P(('group', 'dev')), may hold values from 0 to 31
Outputs:
- adjoint_field: float32 [64, 3, 48, 16, 128], P(('group', 'dev'))
- lattice_grad: float32 [96, 6144], P('dev')
Inputs may be any that keep to these rules, and one draw needn't show every extreme that they name: `conn_lower`: each row names, within the same cluster of 16 blocks, the device index along dev and the slot of the block whose upper face meets this block's lower face (first entry -1 for a wall, then 0 and 0), and 1 in the third entry where that face is reversed along the second grid dimension. A cluster's links form one chain through all its blocks; each link appears mirrored in conn_upper with the same orientation. `conn_upper`: likewise for the block across the upper face, whose lower face it meets. `lengths`: in every cluster some block has 48 active rows and some 48 // 2.
All inputs are finite; a program needn't handle non-finite values.
Results may differ from a plain program's by a relative error of at most 0.0003.
Values sent between devices are 32-bit elements; how exact they have to be, the bound alone decides.
No kernel may reach another device: no remote copies, remote signals or barrier semaphores. Data moves between devices by JAX's collectives and lax.ppermute only.
A program may use at most 64 MiB of HBM per device.

v0:
```python
import math
import jax
import jax.numpy as jnp
from jax import lax
from jax.sharding import PartitionSpec as P

CX = 48
CY = 16
CZ = 128
LX = 96
LY = 64
LZ = 32
SWEEPS = 2
TAPS = [
    (shift_x, shift_y, shift_z, 1.0 / (shift_x * shift_x + shift_y * shift_y + shift_z * shift_z))
    for shift_x in (-1, 0, 1)
    for shift_y in (-1, 0, 1)
    for shift_z in (-1, 0, 1)
    if (shift_x, shift_y, shift_z) != (0, 0, 0)
]
DOMINANCE = 1.25


def stencil(padded, count_x, count_y, count_z):
    running = None
    for shift_x, shift_y, shift_z, factor in TAPS:
        window = padded[
            :,
            1 + shift_x : 1 + shift_x + count_x,
            1 + shift_y : 1 + shift_y + count_y,
            1 + shift_z : 1 + shift_z + count_z,
        ]
        running = factor * window if running is None else running + factor * window
    return running


def extend(values, lower_halo, upper_halo, length):
    zero_row = jnp.zeros_like(lower_halo)[:, None]
    joined = jnp.concatenate([lower_halo[:, None], values, zero_row], axis=1)
    joined = lax.dynamic_update_slice(
        joined, upper_halo[:, None], (jnp.int32(0), length + 1, jnp.int32(0), jnp.int32(0))
    )
    return jnp.pad(joined, ((0, 0), (0, 0), (1, 1), (1, 1)))


def end_faces(values, lengths):
    lower_face = values[:, :, 0]
    upper_face = jax.vmap(
        lambda block_values, length: lax.dynamic_index_in_dim(
            block_values, length - 1, axis=1, keepdims=False
        )
    )(values, lengths)
    return jnp.stack([lower_face, upper_face], axis=1)


def partner_tiles(face_tiles, links, side, slots):
    partner = jnp.maximum(links[:, 0], 0) * slots + links[:, 1]
    chosen = face_tiles[partner, side]
    mirrored = chosen[..., ::-1, :]
    turned = jnp.where((links[:, 2] == 1)[:, None, None, None], mirrored, chosen)
    return jnp.where((links[:, 0] >= 0)[:, None, None, None], turned, jnp.zeros_like(turned))


def hat(coords, points):
    grid_points = jnp.arange(points, dtype=jnp.float32)[None, :, None]
    return jnp.maximum(0.0, 1.0 - jnp.abs(grid_points - coords[:, None, :]))


def on_device(adjoint_seed, stiffness, lengths, conn_lower, conn_upper, coord_x, coord_y, coord_z):
    slots = stiffness.shape[0]
    active = (jnp.arange(CX, dtype=jnp.int32)[None, :] < lengths[:, None]).astype(jnp.float32)[
        :, :, None, None
    ]
    stiff_masked = stiffness * active
    stiff_tiles = lax.all_gather(
        end_faces(stiff_masked[:, None], lengths), "dev", axis=0, tiled=True
    )
    stiff_lower = partner_tiles(stiff_tiles, conn_lower, 1, slots)
    stiff_upper = partner_tiles(stiff_tiles, conn_upper, 0, slots)

    def diagonal_one(stiff_block, lower_halo, upper_halo, length):
        near = stencil(extend(stiff_block[None], lower_halo, upper_halo, length), CX, CY, CZ)[0]
        return DOMINANCE * stiff_block * near

    diagonal = jax.vmap(diagonal_one)(stiff_masked, stiff_lower, stiff_upper, lengths)
    safe = jnp.where(active > 0, diagonal, jnp.ones_like(diagonal))
    source = adjoint_seed.astype(jnp.float32) * active[:, None]
    adjoint = source / safe[:, None]

    def sweep_one(values, low_tile, high_tile, length, stiff_block, source_block, safe_block):
        near = stencil(extend(values, low_tile, high_tile, length), CX, CY, CZ)
        return (source_block + stiff_block[None] * near) / safe_block[None]

    for sweep_index in range(SWEEPS):
        weighted = stiff_masked[:, None] * adjoint
        weighted_tiles = lax.all_gather(end_faces(weighted, lengths), "dev", axis=0, tiled=True)
        lower_halo = partner_tiles(weighted_tiles, conn_lower, 1, slots)
        upper_halo = partner_tiles(weighted_tiles, conn_upper, 0, slots)
        adjoint = jax.vmap(sweep_one)(
            weighted, lower_halo, upper_halo, lengths, stiff_masked, source, safe
        )
    hat_x = hat(coord_x, LX)
    hat_y = hat(coord_y, LY)
    hat_z = hat(coord_z, LZ)
    first = jnp.einsum("bcxyz,bnz->bcxyn", adjoint, hat_z, precision=lax.Precision.HIGHEST)
    second = jnp.einsum("bcxyn,bmy->bxcmn", first, hat_y, precision=lax.Precision.HIGHEST)
    contracted = second.reshape(slots * CX, 3 * LY * LZ)
    hat_rows = jnp.transpose(hat_x, (1, 0, 2)).reshape(LX, slots * CX)
    scale = math.sqrt(
        LX * LY * LZ / (lax.axis_size("group") * lax.axis_size("dev") * slots * CX * CY * CZ)
    )
    partial_value = lax.psum_scatter(
        jnp.dot(
            hat_rows,
            contracted,
            precision=lax.Precision.HIGHEST,
            preferred_element_type=jnp.float32,
        ),
        "dev",
        scatter_dimension=0,
        tiled=True,
    )
    owned = lax.psum(partial_value, "group")
    return (adjoint, owned * scale)


def solution(mesh):
    in_specs = (
        P(("group", "dev"), None, None, None, None),
        P(("group", "dev"), None, None, None),
        P(("group", "dev")),
        P(("group", "dev"), None),
        P(("group", "dev"), None),
        P(("group", "dev"), None),
        P(("group", "dev"), None),
        P(("group", "dev"), None),
    )
    out_specs = (P(("group", "dev"), None, None, None, None), P("dev", None))
    return jax.shard_map(
        on_device, mesh=mesh, in_specs=in_specs, out_specs=out_specs, check_vma=False
    )
```

profile of v0, /device:TPU:0, one launch (start us, length us, event | category | flops | bytes accessed | tf_op | source)
XLA Modules:
  0.0 348.4 jit_solution(1823001275424142487)
XLA Ops:
  7.3 0.7 broadcast_compare_fusion
  8.0 0.7 fusion.188
  8.6 1.3 fusion.204
  11.1 32.6 %all_gather.9 = f32[16,2,1,16,128]{4,3,0,2,1:T(8,128)S(1)} all-gather(f32[2,2,1,16,128]{4,3,0,2,1:T(8,128)S(1)} %pad_maximum_fusion.2), channel_id=1, replica_groups=mesh['group'=4,'dev'=8] {'dev'}, dimensions={0}, use_global_device_ids=true | all-gather | bytes 294912 | tf_op jit(solution)/shard_map/all_gather | solution.py:75
  46.1 15.4 %while.3 = (s32[]{:T(128)}, f32[2,1,50,16,128]{4,3,0,2,1:T(8,128)S(1)}, s32[2,5]{1,0:T(2,128)S(1)}, f32[2,1,1,16,128]{4,3,2,1,0:T(8,128)S(1)}, s32[]{:T(128)}, /*index=5*/s32[5]{0:T(128)S(1)}) while((s32[]{:T(128)}, f32[2,1,50,16,128]{4,3,0,2,1:T(8,128)S(1)}, s32[2,5]{1,0:T(2,128)S(1)}, f32[2,1,1,16,128]{4,3,2,1,0:T(8,128)S(1)}, s32[]{:T(128)}, ...), condition=%wide.while_cond, body=%wide.while_body.sunk | while | flops 2069 | bytes 41215 | solution.py:40
  46.2 0.7 fusion.208
  46.8 3.2 concatenate.70
  50.0 0.7 and_reduce_fusion.6
  50.7 1.3 constant_dynamic-slice_fusion.14
  51.9 1.9 bitcast_dynamic-update-slice_fusion.6
  53.9 0.7 fusion.208
  54.5 3.2 concatenate.70
  57.7 0.7 and_reduce_fusion.6
  58.4 1.3 constant_dynamic-slice_fusion.14
  59.7 1.9 bitcast_dynamic-update-slice_fusion.6
  61.6 4.2 %fusion.142 = f32[2,48,16,128]{3,2,0,1:T(8,128)S(1)} fusion(f32[2,1,50,16,128]{4,3,0,2,1:T(8,128)S(1)} %get-tuple-element.7, pred[2,48]{0,1:T(8,128)(4,1)S(1)} %get-tuple-element.113, f32[2,48]{0,1:T(8,128)S(1)} %get-tuple-element.114, f32[2,48,16,128]{3,2,1,0:T(8,128)S(1)} %copy-done.4), kind=kLoop, calls=%fused_computation.243 | loop fusion | flops 9633792 | bytes 3995648 | tf_op jit(solution)/shard_map/jit(_where)/select_n | solution.py:86
  65.7 1.9 divide_multiply_fusion
  67.7 1.7 copy.85
  69.9 2.2 gather_fusion.7
  72.1 31.7 %all_gather.10 = f32[16,2,3,16,128]{4,3,2,0,1:T(8,128)S(1)} all-gather(f32[2,2,3,16,128]{4,3,2,0,1:T(8,128)S(1)} %pad_maximum_fusion), channel_id=1, replica_groups=mesh['group'=4,'dev'=8] {'dev'}, dimensions={0}, use_global_device_ids=true | all-gather | bytes 884736 | tf_op jit(solution)/shard_map/all_gather | solution.py:96
  105.2 1.9 maximum_maximum_fusion
  107.1 15.0 %while.4 = (s32[]{:T(128)}, f32[2,3,50,16,128]{4,3,1,0,2:T(8,128)S(1)}, s32[2,5]{1,0:T(2,128)S(1)}, f32[2,3,1,16,128]{4,3,2,1,0:T(8,128)S(1)}, s32[]{:T(128)}, /*index=5*/s32[5]{0:T(128)S(1)}) while((s32[]{:T(128)}, f32[2,3,50,16,128]{4,3,1,0,2:T(8,128)S(1)}, s32[2,5]{1,0:T(2,128)S(1)}, f32[2,3,1,16,128]{4,3,2,1,0:T(8,128)S(1)}, s32[]{:T(128)}, ...), condition=%wide.while_cond.1, body=%wide.while_body.1.sunk | while | flops 6165 | bytes 123135 | solution.py:40
  107.1 0.7 fusion.209
  107.8 3.2 concatenate.71
  110.9 0.6 and_reduce_fusion.7
  111.6 1.2 constant_dynamic-slice_fusion.16
  112.7 1.8 bitcast_dynamic-update-slice_fusion.7
  114.6 0.7 fusion.209
  115.2 3.2 concatenate.71
  118.4 0.6 and_reduce_fusion.7
  119.0 1.2 constant_dynamic-slice_fusion.16
  120.2 1.8 bitcast_dynamic-update-slice_fusion.7
  122.1 13.0 %fusion.97 = f32[2,3,48,16,128]{4,3,1,0,2:T(8,128)S(1)} fusion(f32[2,3,50,16,128]{4,3,1,0,2:T(8,128)S(1)} %get-tuple-element.15, f32[2,48,16,128]{3,2,0,1:T(8,128)} %copy-done.2, f32[2,48,16,128]{3,2,0,1:T(8,128)S(1)} %copy_multiply_fusion, f32[2,48]{0,1:T(8,128)S(1)} %get-tuple-element.114, bf16[2,3,48,16,128]{4,3,2,1,0:T(8,128)(2,1)} %param.8), kind=kLoop, calls=%fused_computation.196 | loop fusion | flops 30081024 | bytes 12312576 | tf_op jit(solution)/shard_map/mul | solution.py:95
  135.2 1.2 copy-done.1
  137.0 32.2 %all_gather.11 = f32[16,2,3,16,128]{4,3,2,0,1:T(8,128)S(1)} all-gather(f32[2,2,3,16,128]{4,3,2,0,1:T(8,128)S(1)} %pad_maximum_fusion.1), channel_id=1, replica_groups=mesh['group'=4,'dev'=8] {'dev'}, dimensions={0}, use_global_device_ids=true | all-gather | bytes 884736 | tf_op jit(solution)/shard_map/all_gather | solution.py:96
  170.5 1.9 maximum_maximum_fusion.1
  172.4 15.0 %while.5 = (s32[]{:T(128)}, f32[2,3,50,16,128]{4,3,1,0,2:T(8,128)S(1)}, s32[2,5]{1,0:T(2,128)S(1)}, f32[2,3,1,16,128]{4,3,2,1,0:T(8,128)S(1)}, s32[]{:T(128)}, /*index=5*/s32[5]{0:T(128)S(1)}) while((s32[]{:T(128)}, f32[2,3,50,16,128]{4,3,1,0,2:T(8,128)S(1)}, s32[2,5]{1,0:T(2,128)S(1)}, f32[2,3,1,16,128]{4,3,2,1,0:T(8,128)S(1)}, s32[]{:T(128)}, ...), condition=%wide.while_cond.2, body=%wide.while_body.2.sunk | while | flops 6165 | bytes 123135 | solution.py:40
  172.5 0.7 fusion.210
  173.1 3.2 concatenate.72
  176.3 0.6 and_reduce_fusion.8
  176.9 1.2 constant_dynamic-slice_fusion.18
  178.1 1.8 bitcast_dynamic-update-slice_fusion.8
  179.9 0.7 fusion.210
  180.6 3.2 concatenate.72
  183.8 0.6 and_reduce_fusion.8
  184.4 1.2 constant_dynamic-slice_fusion.18
  185.6 1.8 bitcast_dynamic-update-slice_fusion.8
  187.4 13.0 %fusion.93 = f32[2,3,48,16,128]{4,3,1,0,2:T(8,128)S(1)} fusion(f32[2,3,50,16,128]{4,3,1,0,2:T(8,128)S(1)} %get-tuple-element.23, f32[2,48,16,128]{3,2,0,1:T(8,128)} %copy-done.2, f32[2,48,16,128]{3,2,0,1:T(8,128)S(1)} %copy_multiply_fusion, f32[2,48]{0,1:T(8,128)S(1)} %get-tuple-element.114, bf16[2,3,48,16,128]{4,3,2,1,0:T(8,128)(2,1)} %param.8), kind=kLoop, calls=%fused_computation.190 | loop fusion | flops 29491200 | bytes 12312576 | tf_op jit(solution)/shard_map/vmap()/div | solution.py:92
  200.7 1.4 copy-done.3
  202.1 2.1 fusion.152
  204.2 2.3 copy.98
  206.5 10.4 %convolution_bitcast_fusion = f32[2,48,3,64,32]{3,1,4,2,0:T(8,128)} fusion(f32[2,3,48,16,32]{2,3,4,1,0:T(8,128)} %copy.98, f32[2,16]{1,0:T(2,128)S(1)} %copy-done.5), kind=kOutput, calls=%fused_computation.197 | convolution fusion | flops 113254400 | bytes 2949248 | tf_op jit(solution)/shard_map/bcxyn,bmy->bxcmn/dot_general | solution.py:106
  216.9 9.6 %copy.99 = f32[2,48,3,64,32]{1,0,4,3,2:T(2,128)} copy(f32[2,48,3,64,32]{3,1,4,2,0:T(8,128)} %convolution_bitcast_fusion) | data formatting | bytes 4718592 | tf_op jit(solution)/shard_map/bcxyn,bmy->bxcmn/transpose | solution.py:106
  226.5 6.1 %reshape.97 = f32[96,6144]{0,1:T(8,128)S(1)} reshape(f32[2,48,3,64,32]{1,0,4,3,2:T(2,128)} %copy.99) | data formatting | bytes 4718592 | tf_op jit(solution)/shard_map/reshape | solution.py:107
  232.6 4.7 %fusion.146 = f32[96,6144]{1,0:T(8,128)} fusion(f32[96,6144]{0,1:T(8,128)S(1)} %reshape.97, f32[96]{0:T(128)S(1)} %sub.71), kind=kOutput, calls=%fused_computation.253 | convolution fusion | flops 679514112 | bytes 4718976 | tf_op jit(solution)/shard_map/dot_general | solution.py:113
  237.3 50.6 %fusion = f32[16,6144]{1,0:T(8,128)S(1)} fusion(f32[96,6144]{1,0:T(8,128)} %fusion.146), kind=kCustom, calls=%all-reduce-scatter | all-reduce-scatter fusion | flops 786433 | bytes 2753024
  287.9 4.4 %collective-permute-start = (f32[16,6144]{1,0:T(8,128)S(1)}, f32[16,6144]{1,0:T(8,128)S(1)}, u32[]{:S(2)}, u32[]{:S(2)}) collective-permute-start(f32[16,6144]{1,0:T(8,128)S(1)} %fusion), channel_id=1, source_target_pairs={{0,1},{1,2},{2,3},{3,4},{4,5},{5,6},{6,7},{8,9},{9,10},{10,11},{11... | collective-permute-start | bytes 1179656
  292.4 6.3 %collective-permute-start.1 = (f32[12,6144]{1,0:T(8,128)S(1)}, f32[12,6144]{1,0:T(8,128)S(1)}, u32[]{:S(2)}, u32[]{:S(2)}) collective-permute-start(f32[12,6144]{1,0:T(8,128)S(1)} %slice.489), channel_id=1, source_target_pairs={{0,2},{1,3},{2,4},{3,5},{4,6},{5,7},{8,10},{9,11},{10,12},{11,13},... | collective-permute-start | bytes 884744
  298.7 0.6 dynamic-slice.22
  300.0 4.0 %collective-permute-done.1 = f32[12,6144]{1,0:T(8,128)S(1)} collective-permute-done((f32[12,6144]{1,0:T(8,128)S(1)}, f32[12,6144]{1,0:T(8,128)S(1)}, u32[]{:S(2)}, u32[]{:S(2)}) %collective-permute-start.1) | collective-permute-done | bytes 294944
  304.0 1.0 concatenate.66
  305.0 0.8 constant_dynamic-slice_fusion.6
  305.8 33.9 %all-reduce.9.cloned.1.call-done = f32[12,6144]{1,0:T(8,128)} async-done(((f32[12,6144]{1,0:T(8,128)}), f32[12,6144]{1,0:T(8,128)}) %all-reduce.9.cloned.1.call-update) | async-done | bytes 294928 | tf_op jit(solution)/shard_map/psum | solution.py:123
  339.8 1.8 broadcast_multiply_fusion
  (91 shorter events, 7.7 us)
Async XLA Ops:
  7.2 3.2 copy-start.9
  7.2 3.2 copy-start.4
  7.2 2.9 copy-start.6
  7.2 3.0 copy-start.7
  7.2 332.6 %all-reduce.9.cloned.1.call-start = ((), (), s32[]{:S(2)}) async-start(), calls=%async_computation | async-start | bytes 786432 | tf_op jit(solution)/shard_map/psum | solution.py:123
  9.9 36.0 %copy-start.11 = (s32[4]{0:T(128)S(1)}, s32[4]{0:T(128)}, u32[]{:S(2)}) copy-start(s32[4]{0:T(128)} %constant.25.clone.1) | copy-start | bytes 52
  10.0 36.1 %copy-start.13 = (s32[5]{0:T(128)S(1)}, s32[5]{0:T(128)}, u32[]{:S(2)}) copy-start(s32[5]{0:T(128)} %constant.656) | copy-start | bytes 64
  65.7 2.0 copy-start.2
  67.7 2.2 copy-start
  135.0 1.4 copy-start.1
  200.4 1.6 copy-start.8
  200.7 1.4 copy-start.3
  204.1 2.3 copy-start.5
  226.5 6.1 %copy-start.12 = (f32[2,48]{1,0:T(2,128)S(1)}, f32[2,48]{1,0:T(2,128)}, u32[]{:S(2)}) copy-start(f32[2,48]{1,0:T(2,128)} %param.13) | copy-start | bytes 1156
  237.3 61.4 %copy-start.10 = (u32[32]{0:T(128)S(1)}, u32[32]{0:T(128)}, u32[]{:S(2)}) copy-start(u32[32]{0:T(128)} %constant.342) | copy-start | bytes 388
  287.9 16.0 %collective-permute-start = (f32[16,6144]{1,0:T(8,128)S(1)}, f32[16,6144]{1,0:T(8,128)S(1)}, u32[]{:S(2)}, u32[]{:S(2)}) collective-permute-start(f32[16,6144]{1,0:T(8,128)S(1)} %fusion), channel_id=1, source_target_pairs={{0,1},{1,2},{2,3},{3,4},{4,5},{5,6},{6,7},{8,9},{9,10},{10,11},{11... | collective-permute-start | bytes 1179656
  292.4 11.6 %collective-permute-start.1 = (f32[12,6144]{1,0:T(8,128)S(1)}, f32[12,6144]{1,0:T(8,128)S(1)}, u32[]{:S(2)}, u32[]{:S(2)}) collective-permute-start(f32[12,6144]{1,0:T(8,128)S(1)} %slice.489), channel_id=1, source_target_pairs={{0,2},{1,3},{2,4},{3,5},{4,6},{5,7},{8,10},{9,11},{10,12},{11,13},... | collective-permute-start | bytes 884744
Sparse Core Ops, SparseCore 0:
  306.0 33.7 all-reduce.8
where the time goes:
time: 350 us; the launch traced here: 348 us
  blocking collectives  147 us (42%)
  local copies, waits for them, and re-layouts  63.7 us (18%)
  other arithmetic  56.4 us (16%)
  waiting for transfers between devices  38 us (11%)
  matrix products  17.1 us (5%)
  between operations  15.1 us (4%)
  starting transfers between devices  10.8 us (3%)
    all_gather x2, blocking collectives, on_device(): lax.all_gather(end_faces(weighted, lengths), 'dev', axis=0, tiled=True)  63.9 us
    unnamed x1, blocking collectives  50.6 us
    psum x1, waiting for transfers between devices, on_device(): owned = lax.psum(partial_value, 'group')  33.9 us
    all_gather x1, blocking collectives, on_device(): lax.all_gather(end_faces(stiff_masked[:, None], lengths), 'dev', axis=0,...  32.6 us
    scatter x24, local copies, waits for them, and re-layouts  30.2 us
    scatter x12, other arithmetic  14.9 us
    mul x2, other arithmetic, on_device(): weighted = stiff_masked[:, None] * adjoint  14.9 us
    div x1, other arithmetic, sweep_one(): return (source_block + stiff_block[None] * near) / safe_block[None]  13 us
  transfers between devices with their start and end apart: 3, of which 2 were waited for; matrix products, arithmetic and copies ran while one was open for 0% of the time, Pallas kernels for 0%

commit v1 on v0

--- a/solution.py
+++ b/solution.py
@@ -120,7 +120,7 @@
         scatter_dimension=0,
         tiled=True,
     )
-    owned = lax.psum(partial_value, "group")
+    owned = lax.all_gather(partial_value, "group").sum(axis=0)
     return (adjoint, owned * scale)
 
 

time: 350 us -> 337 us (0.963)
  waiting for transfers between devices: 38 us -> 24.8 us
    psum x1 -> x0, waiting for transfers between devices: 33.9 us -> none  [on_device(): owned = lax.psum(partial_value, 'group')]
    all_gather x0 -> x1, waiting for transfers between devices: none -> 20.8 us  [on_device(): owned = lax.all_gather(partial_value, 'group').sum(axis=0)]
where the time goes in v1:
time: 337 us; the launch traced here: 336 us
  blocking collectives  147 us (44%)
  local copies, waits for them, and re-layouts  63.7 us (19%)
  other arithmetic  56.9 us (17%)
  waiting for transfers between devices  24.8 us (7%)
  matrix products  17.1 us (5%)
  between operations  15.1 us (4%)
  starting transfers between devices  10.8 us (3%)
    all_gather x2, blocking collectives, on_device(): lax.all_gather(end_faces(weighted, lengths), 'dev', axis=0, tiled=True)  63.9 us
    unnamed x1, blocking collectives  50.6 us
    all_gather x1, blocking collectives, on_device(): lax.all_gather(end_faces(stiff_masked[:, None], lengths), 'dev', axis=0,...  32.6 us
    scatter x24, local copies, waits for them, and re-layouts  30.2 us
    all_gather x1, waiting for transfers between devices, on_device(): owned = lax.all_gather(partial_value, 'group').sum(axis=0)  20.8 us
    scatter x12, other arithmetic  14.9 us
    mul x2, other arithmetic, on_device(): weighted = stiff_masked[:, None] * adjoint  14.9 us
    div x1, other arithmetic, sweep_one(): return (source_block + stiff_block[None] * near) / safe_block[None]  13 us
  transfers between devices with their start and end apart: 3, of which 2 were waited for; matrix products, arithmetic and copies ran while one was open for 0% of the time, Pallas kernels for 0%

profile of v1, /device:TPU:0, one launch (start us, length us, event | category | flops | bytes accessed | tf_op | source)
XLA Modules:
  0.0 335.8 jit_solution(13834892080746963850)
XLA Ops:
  7.3 0.7 broadcast_compare_fusion
  8.0 0.7 fusion.188
  8.6 1.3 fusion.204
  11.1 32.6 %all_gather.15 = f32[16,2,1,16,128]{4,3,0,2,1:T(8,128)S(1)} all-gather(f32[2,2,1,16,128]{4,3,0,2,1:T(8,128)S(1)} %pad_maximum_fusion.2), channel_id=1, replica_groups=mesh['group'=4,'dev'=8] {'dev'}, dimensions={0}, use_global_device_ids=true | all-gather | bytes 294912 | tf_op jit(solution)/shard_map/all_gather | solution.py:75
  46.1 15.4 %while.3 = (s32[]{:T(128)}, f32[2,1,50,16,128]{4,3,0,2,1:T(8,128)S(1)}, s32[2,5]{1,0:T(2,128)S(1)}, f32[2,1,1,16,128]{4,3,2,1,0:T(8,128)S(1)}, s32[]{:T(128)}, /*index=5*/s32[5]{0:T(128)S(1)}) while((s32[]{:T(128)}, f32[2,1,50,16,128]{4,3,0,2,1:T(8,128)S(1)}, s32[2,5]{1,0:T(2,128)S(1)}, f32[2,1,1,16,128]{4,3,2,1,0:T(8,128)S(1)}, s32[]{:T(128)}, ...), condition=%wide.while_cond, body=%wide.while_body.sunk | while | flops 2069 | bytes 41215 | solution.py:40
  46.2 0.7 fusion.208
  46.8 3.2 concatenate.70
  50.0 0.7 and_reduce_fusion.6
  50.7 1.3 constant_dynamic-slice_fusion.13
  51.9 1.9 bitcast_dynamic-update-slice_fusion.6
  53.9 0.7 fusion.208
  54.5 3.2 concatenate.70
  57.7 0.7 and_reduce_fusion.6
  58.4 1.3 constant_dynamic-slice_fusion.13
  59.7 1.9 bitcast_dynamic-update-slice_fusion.6
  61.6 4.2 %fusion.142 = f32[2,48,16,128]{3,2,0,1:T(8,128)S(1)} fusion(f32[2,1,50,16,128]{4,3,0,2,1:T(8,128)S(1)} %get-tuple-element.7, pred[2,48]{0,1:T(8,128)(4,1)S(1)} %get-tuple-element.113, f32[2,48]{0,1:T(8,128)S(1)} %get-tuple-element.114, f32[2,48,16,128]{3,2,1,0:T(8,128)S(1)} %copy-done.4), kind=kLoop, calls=%fused_computation.243 | loop fusion | flops 9633792 | bytes 3995648 | tf_op jit(solution)/shard_map/jit(_where)/select_n | solution.py:86
  65.7 1.9 divide_multiply_fusion
  67.7 1.7 copy.85
  69.9 2.2 gather_fusion.7
  72.1 31.7 %all_gather.16 = f32[16,2,3,16,128]{4,3,2,0,1:T(8,128)S(1)} all-gather(f32[2,2,3,16,128]{4,3,2,0,1:T(8,128)S(1)} %pad_maximum_fusion), channel_id=1, replica_groups=mesh['group'=4,'dev'=8] {'dev'}, dimensions={0}, use_global_device_ids=true | all-gather | bytes 884736 | tf_op jit(solution)/shard_map/all_gather | solution.py:96
  105.2 1.9 maximum_maximum_fusion
  107.1 15.0 %while.4 = (s32[]{:T(128)}, f32[2,3,50,16,128]{4,3,1,0,2:T(8,128)S(1)}, s32[2,5]{1,0:T(2,128)S(1)}, f32[2,3,1,16,128]{4,3,2,1,0:T(8,128)S(1)}, s32[]{:T(128)}, /*index=5*/s32[5]{0:T(128)S(1)}) while((s32[]{:T(128)}, f32[2,3,50,16,128]{4,3,1,0,2:T(8,128)S(1)}, s32[2,5]{1,0:T(2,128)S(1)}, f32[2,3,1,16,128]{4,3,2,1,0:T(8,128)S(1)}, s32[]{:T(128)}, ...), condition=%wide.while_cond.1, body=%wide.while_body.1.sunk | while | flops 6165 | bytes 123135 | solution.py:40
  107.1 0.7 fusion.209
  107.8 3.2 concatenate.71
  110.9 0.6 and_reduce_fusion.7
  111.6 1.2 constant_dynamic-slice_fusion.15
  112.7 1.8 bitcast_dynamic-update-slice_fusion.7
  114.6 0.7 fusion.209
  115.2 3.2 concatenate.71
  118.4 0.6 and_reduce_fusion.7
  119.0 1.2 constant_dynamic-slice_fusion.15
  120.2 1.8 bitcast_dynamic-update-slice_fusion.7
  122.1 13.0 %fusion.97 = f32[2,3,48,16,128]{4,3,1,0,2:T(8,128)S(1)} fusion(f32[2,3,50,16,128]{4,3,1,0,2:T(8,128)S(1)} %get-tuple-element.15, f32[2,48,16,128]{3,2,0,1:T(8,128)} %copy-done.2, f32[2,48,16,128]{3,2,0,1:T(8,128)S(1)} %copy_multiply_fusion, f32[2,48]{0,1:T(8,128)S(1)} %get-tuple-element.114, bf16[2,3,48,16,128]{4,3,2,1,0:T(8,128)(2,1)} %param.8), kind=kLoop, calls=%fused_computation.196 | loop fusion | flops 30081024 | bytes 12312576 | tf_op jit(solution)/shard_map/mul | solution.py:95
  135.2 1.2 copy-done.1
  137.0 32.2 %all_gather.17 = f32[16,2,3,16,128]{4,3,2,0,1:T(8,128)S(1)} all-gather(f32[2,2,3,16,128]{4,3,2,0,1:T(8,128)S(1)} %pad_maximum_fusion.1), channel_id=1, replica_groups=mesh['group'=4,'dev'=8] {'dev'}, dimensions={0}, use_global_device_ids=true | all-gather | bytes 884736 | tf_op jit(solution)/shard_map/all_gather | solution.py:96
  170.5 1.9 maximum_maximum_fusion.1
  172.4 15.0 %while.5 = (s32[]{:T(128)}, f32[2,3,50,16,128]{4,3,1,0,2:T(8,128)S(1)}, s32[2,5]{1,0:T(2,128)S(1)}, f32[2,3,1,16,128]{4,3,2,1,0:T(8,128)S(1)}, s32[]{:T(128)}, /*index=5*/s32[5]{0:T(128)S(1)}) while((s32[]{:T(128)}, f32[2,3,50,16,128]{4,3,1,0,2:T(8,128)S(1)}, s32[2,5]{1,0:T(2,128)S(1)}, f32[2,3,1,16,128]{4,3,2,1,0:T(8,128)S(1)}, s32[]{:T(128)}, ...), condition=%wide.while_cond.2, body=%wide.while_body.2.sunk | while | flops 6165 | bytes 123135 | solution.py:40
  172.5 0.7 fusion.210
  173.1 3.2 concatenate.72
  176.3 0.6 and_reduce_fusion.8
  176.9 1.2 constant_dynamic-slice_fusion.17
  178.1 1.8 bitcast_dynamic-update-slice_fusion.8
  179.9 0.7 fusion.210
  180.6 3.2 concatenate.72
  183.8 0.6 and_reduce_fusion.8
  184.4 1.2 constant_dynamic-slice_fusion.17
  185.6 1.8 bitcast_dynamic-update-slice_fusion.8
  187.4 13.0 %fusion.93 = f32[2,3,48,16,128]{4,3,1,0,2:T(8,128)S(1)} fusion(f32[2,3,50,16,128]{4,3,1,0,2:T(8,128)S(1)} %get-tuple-element.23, f32[2,48,16,128]{3,2,0,1:T(8,128)} %copy-done.2, f32[2,48,16,128]{3,2,0,1:T(8,128)S(1)} %copy_multiply_fusion, f32[2,48]{0,1:T(8,128)S(1)} %get-tuple-element.114, bf16[2,3,48,16,128]{4,3,2,1,0:T(8,128)(2,1)} %param.8), kind=kLoop, calls=%fused_computation.190 | loop fusion | flops 29491200 | bytes 12312576 | tf_op jit(solution)/shard_map/vmap()/div | solution.py:92
  200.7 1.4 copy-done.3
  202.1 2.1 fusion.152
  204.2 2.3 copy.98
  206.5 10.4 %convolution_bitcast_fusion = f32[2,48,3,64,32]{3,1,4,2,0:T(8,128)} fusion(f32[2,3,48,16,32]{2,3,4,1,0:T(8,128)} %copy.98, f32[2,16]{1,0:T(2,128)S(1)} %copy-done.5), kind=kOutput, calls=%fused_computation.197 | convolution fusion | flops 113254400 | bytes 2949248 | tf_op jit(solution)/shard_map/bcxyn,bmy->bxcmn/dot_general | solution.py:106
  216.9 9.6 %copy.99 = f32[2,48,3,64,32]{1,0,4,3,2:T(2,128)} copy(f32[2,48,3,64,32]{3,1,4,2,0:T(8,128)} %convolution_bitcast_fusion) | data formatting | bytes 4718592 | tf_op jit(solution)/shard_map/bcxyn,bmy->bxcmn/transpose | solution.py:106
  226.5 6.1 %reshape.97 = f32[96,6144]{0,1:T(8,128)S(1)} reshape(f32[2,48,3,64,32]{1,0,4,3,2:T(2,128)} %copy.99) | data formatting | bytes 4718592 | tf_op jit(solution)/shard_map/reshape | solution.py:107
  232.6 4.7 %fusion.146 = f32[96,6144]{1,0:T(8,128)} fusion(f32[96,6144]{0,1:T(8,128)S(1)} %reshape.97, f32[96]{0:T(128)S(1)} %sub.71), kind=kOutput, calls=%fused_computation.254 | convolution fusion | flops 679514112 | bytes 4718976 | tf_op jit(solution)/shard_map/dot_general | solution.py:113
  237.3 50.6 %fusion = f32[16,6144]{1,0:T(8,128)S(1)} fusion(f32[96,6144]{1,0:T(8,128)} %fusion.146), kind=kCustom, calls=%all-reduce-scatter | all-reduce-scatter fusion | flops 786433 | bytes 2753024
  287.9 4.4 %collective-permute-start = (f32[16,6144]{1,0:T(8,128)S(1)}, f32[16,6144]{1,0:T(8,128)S(1)}, u32[]{:S(2)}, u32[]{:S(2)}) collective-permute-start(f32[16,6144]{1,0:T(8,128)S(1)} %fusion), channel_id=1, source_target_pairs={{0,1},{1,2},{2,3},{3,4},{4,5},{5,6},{6,7},{8,9},{9,10},{10,11},{11... | collective-permute-start | bytes 1179656
  292.4 6.3 %collective-permute-start.1 = (f32[12,6144]{1,0:T(8,128)S(1)}, f32[12,6144]{1,0:T(8,128)S(1)}, u32[]{:S(2)}, u32[]{:S(2)}) collective-permute-start(f32[12,6144]{1,0:T(8,128)S(1)} %slice.489), channel_id=1, source_target_pairs={{0,2},{1,3},{2,4},{3,5},{4,6},{5,7},{8,10},{9,11},{10,12},{11,13},... | collective-permute-start | bytes 884744
  300.0 4.0 %collective-permute-done.1 = f32[12,6144]{1,0:T(8,128)S(1)} collective-permute-done((f32[12,6144]{1,0:T(8,128)S(1)}, f32[12,6144]{1,0:T(8,128)S(1)}, u32[]{:S(2)}, u32[]{:S(2)}) %collective-permute-start.1) | collective-permute-done | bytes 294944
  304.0 1.0 concatenate.66
  305.0 0.8 dynamic-slice_bitcast_fusion
  305.8 20.8 %all-gather.4.cloned.1.call-done = f32[4,12,6144]{2,1,0:T(8,128)} async-done(((f32[1,12,6144]{2,1,0:T(8,128)}), f32[4,12,6144]{2,1,0:T(8,128)}) %all-gather.4.cloned.1.call-update) | async-done | bytes 1179664 | tf_op jit(solution)/shard_map/all_gather | solution.py:123
  326.6 1.5 reduce_sum.9
  328.2 0.8 broadcast_multiply_fusion
  (92 shorter events, 8.3 us)
Async XLA Ops:
  7.2 3.2 copy-start.9
  7.2 3.2 copy-start.4
  7.2 2.9 copy-start.6
  7.2 3.0 copy-start.7
  7.2 319.4 %all-gather.4.cloned.1.call-start = ((), (), s32[]{:S(2)}) async-start(), calls=%async_computation | async-start | bytes 1966080 | tf_op jit(solution)/shard_map/all_gather | solution.py:123
  9.9 36.0 %copy-start.11 = (s32[4]{0:T(128)S(1)}, s32[4]{0:T(128)}, u32[]{:S(2)}) copy-start(s32[4]{0:T(128)} %constant.25.clone.1) | copy-start | bytes 52
  10.0 36.1 %copy-start.13 = (s32[5]{0:T(128)S(1)}, s32[5]{0:T(128)}, u32[]{:S(2)}) copy-start(s32[5]{0:T(128)} %constant.657) | copy-start | bytes 64
  65.7 2.0 copy-start.2
  67.7 2.2 copy-start
  135.0 1.4 copy-start.1
  200.4 1.6 copy-start.8
  200.7 1.4 copy-start.3
  204.1 2.3 copy-start.5
  226.5 6.1 %copy-start.12 = (f32[2,48]{1,0:T(2,128)S(1)}, f32[2,48]{1,0:T(2,128)}, u32[]{:S(2)}) copy-start(f32[2,48]{1,0:T(2,128)} %param.13) | copy-start | bytes 1156
  237.3 61.4 %copy-start.10 = (u32[32]{0:T(128)S(1)}, u32[32]{0:T(128)}, u32[]{:S(2)}) copy-start(u32[32]{0:T(128)} %constant.343) | copy-start | bytes 388
  287.9 16.0 %collective-permute-start = (f32[16,6144]{1,0:T(8,128)S(1)}, f32[16,6144]{1,0:T(8,128)S(1)}, u32[]{:S(2)}, u32[]{:S(2)}) collective-permute-start(f32[16,6144]{1,0:T(8,128)S(1)} %fusion), channel_id=1, source_target_pairs={{0,1},{1,2},{2,3},{3,4},{4,5},{5,6},{6,7},{8,9},{9,10},{10,11},{11... | collective-permute-start | bytes 1179656
  292.4 11.6 %collective-permute-start.1 = (f32[12,6144]{1,0:T(8,128)S(1)}, f32[12,6144]{1,0:T(8,128)S(1)}, u32[]{:S(2)}, u32[]{:S(2)}) collective-permute-start(f32[12,6144]{1,0:T(8,128)S(1)} %slice.489), channel_id=1, source_target_pairs={{0,2},{1,3},{2,4},{3,5},{4,6},{5,7},{8,10},{9,11},{10,12},{11,13},... | collective-permute-start | bytes 884744
Sparse Core Ops, SparseCore 0:
  306.0 20.5 all-gather.3
